TPU v7x, 32 devices: a whole 2x2x4 slice. The times are simulated.
32 devices in a mesh: dp: 4 (over z), ctx: 8 (over y, x, core).
Axes of the slice: x: 2, y: 2, z: 4, core: 2. Of those that a mesh axis runs over, the one named last changes fastest.
Arguments:
- tokens: bfloat16 [4, 1024, 8192], P('dp', 'ctx'), may hold values from -6 to 6
- w_down: bfloat16 [8192, 512], P(('dp', 'ctx')), may hold values from -0.0625 to 0.0625
- w_up: bfloat16 [512, 1024], replicated, may hold values from -0.25 to 0.25
- queries: bfloat16 [4, 1024, 4096], P('dp', 'ctx'), may hold values from -70 to 70, as said below
- block_order: int32 [4, 16], P('dp', 'ctx'), may hold values from 0 to 15, each once within a row
Outputs:
- attended: bfloat16 [4, 1024, 4096], P('dp', 'ctx')
Inputs may be any that keep to these rules, and one draw needn't show every extreme that they name: `queries`: query entries.
All inputs are finite; a program needn't handle non-finite values.
Results may differ from a plain program's by a relative error of at most 0.014.
The roundings to bfloat16 on the way count: a program that leaves them out, or rounds other values in their place, can miss the bound.
Values may be sent and summed in bfloat16 or wider, within the bound.
A program may use at most 64 MiB of HBM per device.

v0:
```python
import math
import jax
import jax.numpy as jnp
from jax import lax
from jax.sharding import PartitionSpec as P

QH = 32
KVH = 4
HD = 128


def per_device(tokens, w_down, w_up, queries, block_order):
    local_rows = tokens.shape[1]
    half_rows = local_rows // 2
    features = tokens[0]
    summed = jnp.dot(
        features,
        lax.all_gather(w_down, ("dp", "ctx"), axis=0, tiled=True),
        preferred_element_type=jnp.float32,
    )
    latent = summed.astype(jnp.bfloat16)
    order_whole = lax.all_gather(block_order, "ctx", axis=1, tiled=True)[0]
    block_count = order_whole.shape[0]
    local_ids = jnp.arange(local_rows, dtype=jnp.int32)
    query_pos = (
        jnp.where(local_ids < half_rows, block_order[0, 0], block_order[0, 1]) * half_rows
        + local_ids % half_rows
    )
    group = QH // KVH
    query_heads = queries[0].reshape(local_rows, KVH, group, HD).transpose(1, 2, 0, 3)
    score_scale = HD ** (-0.5)

    def update(carry, kv_block, key_pos):
        running_max, running_total, running_sum = carry
        width = kv_block.shape[0]
        key_block = kv_block[:, : KVH * HD].reshape(width, KVH, HD)
        value_block = kv_block[:, KVH * HD :].reshape(width, KVH, HD)
        scores = (
            jnp.einsum("kgsd,tkd->kgst", query_heads, key_block, preferred_element_type=jnp.float32)
            * score_scale
        )
        allowed = key_pos[None, :] <= query_pos[:, None]
        scores = jnp.where(allowed, scores, -1e30)
        new_max = jnp.maximum(running_max, jnp.max(scores, axis=-1))
        correction = jnp.exp(running_max - new_max)
        expo = jnp.where(allowed, jnp.exp(scores - new_max[..., None]), 0.0)
        new_total = running_total * correction + jnp.sum(expo, axis=-1)
        contrib = jnp.einsum(
            "kgst,tkd->kgsd",
            expo.astype(jnp.bfloat16),
            value_block,
            preferred_element_type=jnp.float32,
        )
        return (new_max, new_total, running_sum * correction[..., None] + contrib)

    start_state = (
        jnp.full((KVH, group, local_rows), -1e30, jnp.float32),
        jnp.zeros((KVH, group, local_rows), jnp.float32),
        jnp.zeros((KVH, group, local_rows, HD), jnp.float32),
    )
    kv_local = jnp.dot(latent, w_up, preferred_element_type=jnp.float32).astype(jnp.bfloat16)
    piece = lax.all_gather(kv_local, "ctx", axis=0, tiled=True)
    count = piece.shape[0]
    width = math.gcd(count, 256)
    blocks = piece.reshape(count // width, width, piece.shape[1])
    row_ids = jnp.arange(count, dtype=jnp.int32)
    onehot = (row_ids // half_rows)[:, None] == jnp.arange(block_count, dtype=jnp.int32)[None, :]
    block_ids = jnp.sum(jnp.where(onehot, order_whole[None, :], 0), axis=1)
    key_positions = (block_ids * half_rows + row_ids % half_rows).reshape(count // width, width)

    def step_block(state, inputs):
        block, key_pos = inputs
        state = update(state, block, key_pos)
        return (state, None)

    result, unused = lax.scan(step_block, start_state, (blocks, key_positions))
    unused_max, final_total, final_sum = result
    outputs = final_sum / final_total[..., None]
    return outputs.transpose(2, 0, 1, 3).reshape(1, local_rows, QH * HD).astype(jnp.bfloat16)


def solution(mesh):
    placed = (
        P("dp", "ctx", None),
        P(("dp", "ctx"), None),
        P(),
        P("dp", "ctx", None),
        P("dp", "ctx"),
    )
    return jax.shard_map(
        per_device, mesh=mesh, in_specs=placed, out_specs=P("dp", "ctx", None), check_vma=False
    )
```

profile of v0, /device:TPU:0, one launch (start us, length us, event | category | flops | bytes accessed | tf_op | source)
XLA Modules:
  0.0 171.8 jit_solution(13662498133776428902)
XLA Ops:
  6.5 0.7 all-gather.3.cloned.1.call-update
  7.3 0.0 all-gather.5.cloned.1.call-start
  7.3 83.1 %all-gather.3.cloned.1.call-done = bf16[8192,512]{1,0:T(8,128)(2,1)} async-done(((bf16[256,512]{1,0:T(8,128)(2,1)}), bf16[8192,512]{1,0:T(8,128)(2,1)}) %all-gather.3.cloned.1.call-update) | async-done | bytes 8388624 | tf_op jit(solution)/shard_map/all_gather | solution.py:18
  90.4 5.8 %convolution_convert_fusion = bf16[128,1024]{1,0:T(8,128)(2,1)} fusion(bf16[512,1024]{1,0:T(8,128)(2,1)} %param.9, bf16[8192,512]{1,0:T(8,128)(2,1)} %all-gather.3.cloned.1.call-done, bf16[1,128,8192]{2,1,0:T(8,128)(2,1)S(1)} %copy-done), kind=kOutput, calls=%fused_computation.31 | convolution fusion | flops 1208156160 | bytes 11796480 | tf_op jit(solution)/shard_map/dot_general | solution.py:61
  96.3 0.6 dynamic-slice
  97.6 0.1 bitcast_dynamic-update-slice_fusion
  97.7 7.3 %all-reduce = s32[16]{0:T(128)S(1)} all-reduce(s32[16]{0:T(128)S(1)} %bitcast_dynamic-update-slice_fusion), channel_id=1, replica_groups=mesh['dp'=4,'ctx'=8] {'ctx'}, use_global_device_ids=true, to_apply=%add | all-reduce | flops 16 | bytes 128
  105.0 0.1 select_reduce_fusion
  105.1 1.6 copy.18
  106.7 1.3 copy.20
  108.0 0.6 fusion.35
  108.7 14.3 %all-gather.5.cloned.1.call-done = bf16[1024,1024]{1,0:T(8,128)(2,1)} async-done(((bf16[128,1024]{1,0:T(8,128)(2,1)}), bf16[1024,1024]{1,0:T(8,128)(2,1)}) %all-gather.5.cloned.1.call-update) | async-done | bytes 2097168 | tf_op jit(solution)/shard_map/all_gather | solution.py:62
  122.9 38.1 %while.15 = (s32[]{:T(128)}, f32[4,8,128]{2,1,0:T(8,128)S(1)}, f32[4,8,128]{2,1,0:T(8,128)S(1)}, f32[4,8,128,128]{3,2,1,0:T(8,128)}, s32[4,256]{1,0:T(4,128)S(1)...) while((s32[]{:T(128)}, f32[4,8,128]{2,1,0:T(8,128)S(1)}, ...), condition=%wide.region_4.5_spmd.clone, body=%wide.region_1.4_spmd.clone.sunk | while | flops 552129792 | bytes 38670536 | solution.py:76
  122.9 1.3 fusion.55
  124.2 0.1 broadcast_compare_fusion.2
  124.3 1.1 constant_dynamic-slice_fusion.5
  125.4 0.2 copy.31
  125.7 2.2 %fusion.57 = (f32[4,8,128]{2,1,0:T(8,128)S(1)}, f32[4,256,8,128]{3,1,2,0:T(8,128)S(1)}) fusion(pred[128,256]{0,1:T(8,128)(4,1)S(1)} %broadcast_compare_fusion.2, bf16[256,4,128,1]{0,2,3,1:T(8,128)(2,1)S(1)} %bitcast.71, bf16[4,8,128,128]{3,2,1,0:T(8,128)(2,1)} %get-tuple-element.223), kind=kOutput, calls=%fused_computation.3.clone.1 | convolution fusion | flops 271577088 | bytes 5554176 | tf_op jit(solution)/shard_map/while/body/eval_jaxpr/kgsd,tkd->kgst/dot_general | solution.py:39
  127.9 1.1 fusion.58
  129.0 2.1 %fusion.60 = f32[4,8,128,128]{3,2,1,0:T(8,128)S(1)} fusion(f32[4,8,128,128]{3,2,1,0:T(8,128)S(1)} %copy-done.1, bf16[256,4,128,1]{0,2,3,1:T(8,128)(2,1)S(1)} %bitcast.72, f32[4,256,8,128]{3,1,2,0:T(8,128)S(1)} %get-tuple-element.191, f32[4,8,128]{2,1,0:T(8,128)S(1)} %select_maximum_fusion.2, pred[128,256]{0,1:T(8,128)(4,1)S(1)} %broadcast_compare_fusion.2, ...), kind=kOutput, calls=%fused_computation.8.clone.1 | convolution fusion | flops 275251200 | bytes 8716289 | tf_op jit(solution)/shard_map/while/body/eval_jaxpr/kgst,tkd->kgsd/dot_general | solution.py:48
  131.2 1.3 copy-done.2
  132.5 1.3 fusion.55
  133.8 0.1 broadcast_compare_fusion.2
  133.9 1.1 constant_dynamic-slice_fusion.5
  135.0 0.2 copy.31
  135.2 2.2 %fusion.57 = (f32[4,8,128]{2,1,0:T(8,128)S(1)}, f32[4,256,8,128]{3,1,2,0:T(8,128)S(1)}) fusion(pred[128,256]{0,1:T(8,128)(4,1)S(1)} %broadcast_compare_fusion.2, bf16[256,4,128,1]{0,2,3,1:T(8,128)(2,1)S(1)} %bitcast.71, bf16[4,8,128,128]{3,2,1,0:T(8,128)(2,1)} %get-tuple-element.223), kind=kOutput, calls=%fused_computation.3.clone.1 | convolution fusion | flops 271577088 | bytes 5554176 | tf_op jit(solution)/shard_map/while/body/eval_jaxpr/kgsd,tkd->kgst/dot_general | solution.py:39
  137.5 1.1 fusion.58
  138.6 2.1 %fusion.60 = f32[4,8,128,128]{3,2,1,0:T(8,128)S(1)} fusion(f32[4,8,128,128]{3,2,1,0:T(8,128)S(1)} %copy-done.1, bf16[256,4,128,1]{0,2,3,1:T(8,128)(2,1)S(1)} %bitcast.72, f32[4,256,8,128]{3,1,2,0:T(8,128)S(1)} %get-tuple-element.191, f32[4,8,128]{2,1,0:T(8,128)S(1)} %select_maximum_fusion.2, pred[128,256]{0,1:T(8,128)(4,1)S(1)} %broadcast_compare_fusion.2, ...), kind=kOutput, calls=%fused_computation.8.clone.1 | convolution fusion | flops 275251200 | bytes 8716289 | tf_op jit(solution)/shard_map/while/body/eval_jaxpr/kgst,tkd->kgsd/dot_general | solution.py:48
  140.7 1.3 copy-done.2
  142.0 1.3 fusion.55
  143.3 0.1 broadcast_compare_fusion.2
  143.4 1.1 constant_dynamic-slice_fusion.5
  144.5 0.2 copy.31
  144.8 2.2 %fusion.57 = (f32[4,8,128]{2,1,0:T(8,128)S(1)}, f32[4,256,8,128]{3,1,2,0:T(8,128)S(1)}) fusion(pred[128,256]{0,1:T(8,128)(4,1)S(1)} %broadcast_compare_fusion.2, bf16[256,4,128,1]{0,2,3,1:T(8,128)(2,1)S(1)} %bitcast.71, bf16[4,8,128,128]{3,2,1,0:T(8,128)(2,1)} %get-tuple-element.223), kind=kOutput, calls=%fused_computation.3.clone.1 | convolution fusion | flops 271577088 | bytes 5554176 | tf_op jit(solution)/shard_map/while/body/eval_jaxpr/kgsd,tkd->kgst/dot_general | solution.py:39
  147.0 1.1 fusion.58
  148.1 2.1 %fusion.60 = f32[4,8,128,128]{3,2,1,0:T(8,128)S(1)} fusion(f32[4,8,128,128]{3,2,1,0:T(8,128)S(1)} %copy-done.1, bf16[256,4,128,1]{0,2,3,1:T(8,128)(2,1)S(1)} %bitcast.72, f32[4,256,8,128]{3,1,2,0:T(8,128)S(1)} %get-tuple-element.191, f32[4,8,128]{2,1,0:T(8,128)S(1)} %select_maximum_fusion.2, pred[128,256]{0,1:T(8,128)(4,1)S(1)} %broadcast_compare_fusion.2, ...), kind=kOutput, calls=%fused_computation.8.clone.1 | convolution fusion | flops 275251200 | bytes 8716289 | tf_op jit(solution)/shard_map/while/body/eval_jaxpr/kgst,tkd->kgsd/dot_general | solution.py:48
  150.2 1.3 copy-done.2
  151.5 1.3 fusion.55
  152.8 0.1 broadcast_compare_fusion.2
  152.9 1.1 constant_dynamic-slice_fusion.5
  154.0 0.2 copy.31
  154.3 2.2 %fusion.57 = (f32[4,8,128]{2,1,0:T(8,128)S(1)}, f32[4,256,8,128]{3,1,2,0:T(8,128)S(1)}) fusion(pred[128,256]{0,1:T(8,128)(4,1)S(1)} %broadcast_compare_fusion.2, bf16[256,4,128,1]{0,2,3,1:T(8,128)(2,1)S(1)} %bitcast.71, bf16[4,8,128,128]{3,2,1,0:T(8,128)(2,1)} %get-tuple-element.223), kind=kOutput, calls=%fused_computation.3.clone.1 | convolution fusion | flops 271577088 | bytes 5554176 | tf_op jit(solution)/shard_map/while/body/eval_jaxpr/kgsd,tkd->kgst/dot_general | solution.py:39
  156.5 1.1 fusion.58
  157.6 2.1 %fusion.60 = f32[4,8,128,128]{3,2,1,0:T(8,128)S(1)} fusion(f32[4,8,128,128]{3,2,1,0:T(8,128)S(1)} %copy-done.1, bf16[256,4,128,1]{0,2,3,1:T(8,128)(2,1)S(1)} %bitcast.72, f32[4,256,8,128]{3,1,2,0:T(8,128)S(1)} %get-tuple-element.191, f32[4,8,128]{2,1,0:T(8,128)S(1)} %select_maximum_fusion.2, pred[128,256]{0,1:T(8,128)(4,1)S(1)} %broadcast_compare_fusion.2, ...), kind=kOutput, calls=%fused_computation.8.clone.1 | convolution fusion | flops 275251200 | bytes 8716289 | tf_op jit(solution)/shard_map/while/body/eval_jaxpr/kgst,tkd->kgsd/dot_general | solution.py:48
  159.7 1.3 copy-done.2
  161.0 1.9 %fusion.28 = bf16[128,4,8,128]{3,0,2,1:T(8,128)(2,1)S(1)} fusion(f32[4,8,128,128]{3,2,1,0:T(8,128)} %get-tuple-element.48, f32[4,8,128]{2,1,0:T(8,128)S(1)} %get-tuple-element.49), kind=kLoop, calls=%fused_computation.33 | loop fusion | flops 1048576 | bytes 3162112 | tf_op jit(solution)/shard_map/convert_element_type | solution.py:79
  163.0 0.7 copy.21
  163.7 1.3 convert_element_type.30
  (48 shorter events, 0.4 us)
Async XLA Ops:
  6.5 83.9 %copy-start = (bf16[1,128,8192]{2,1,0:T(8,128)(2,1)S(1)}, bf16[1,128,8192]{2,1,0:T(8,128)(2,1)}, u32[]{:S(2)}) copy-start(bf16[1,128,8192]{2,1,0:T(8,128)(2,1)} %param.7) | copy-start | bytes 6291460
  6.5 83.9 %all-gather.3.cloned.1.call-start = ((), (), s32[]{:S(2)}) async-start(), calls=%async_computation | async-start | bytes 8650752 | tf_op jit(solution)/shard_map/all_gather | solution.py:18
  7.3 89.0 %copy-start.4 = (u32[32]{0:T(128)S(1)}, u32[32]{0:T(128)}, u32[]{:S(2)}) copy-start(u32[32]{0:T(128)} %constant.71) | copy-start | bytes 388
  7.3 90.3 %copy-start.3 = (s32[1,2]{1,0:T(1,128)S(1)}, s32[1,2]{1,0:T(1,128)}, u32[]{:S(2)}) copy-start(s32[1,2]{1,0:T(1,128)} %param.11) | copy-start | bytes 28
  7.3 115.6 %all-gather.5.cloned.1.call-start = ((), (), s32[]{:S(2)}) async-start(), calls=%async_computation.1 | async-start | bytes 2359296 | tf_op jit(solution)/shard_map/all_gather | solution.py:62
  125.7 3.3 %copy-start.1 = (f32[4,8,128,128]{3,2,1,0:T(8,128)S(1)}, f32[4,8,128,128]{3,2,1,0:T(8,128)}, u32[]{:S(2)}) copy-start(f32[4,8,128,128]{3,2,1,0:T(8,128)} %get-tuple-element.209) | copy-start | bytes 6291460 | tf_op jit(solution)/shard_map/while
  131.2 1.3 copy-start.2
  135.2 3.3 %copy-start.1 = (f32[4,8,128,128]{3,2,1,0:T(8,128)S(1)}, f32[4,8,128,128]{3,2,1,0:T(8,128)}, u32[]{:S(2)}) copy-start(f32[4,8,128,128]{3,2,1,0:T(8,128)} %get-tuple-element.209) | copy-start | bytes 6291460 | tf_op jit(solution)/shard_map/while
  140.7 1.3 copy-start.2
  144.7 3.3 %copy-start.1 = (f32[4,8,128,128]{3,2,1,0:T(8,128)S(1)}, f32[4,8,128,128]{3,2,1,0:T(8,128)}, u32[]{:S(2)}) copy-start(f32[4,8,128,128]{3,2,1,0:T(8,128)} %get-tuple-element.209) | copy-start | bytes 6291460 | tf_op jit(solution)/shard_map/while
  150.2 1.3 copy-start.2
  154.3 3.3 %copy-start.1 = (f32[4,8,128,128]{3,2,1,0:T(8,128)S(1)}, f32[4,8,128,128]{3,2,1,0:T(8,128)}, u32[]{:S(2)}) copy-start(f32[4,8,128,128]{3,2,1,0:T(8,128)} %get-tuple-element.209) | copy-start | bytes 6291460 | tf_op jit(solution)/shard_map/while
  159.7 1.3 copy-start.2
Sparse Core Ops, SparseCore 0:
  10.2 80.1 all-gather.2
  96.4 26.4 all-gather.4
where the time goes:
time: 172 us
  waiting for transfers between devices  98.1 us (57%)
  matrix products  23.1 us (13%)
  local copies, waits for them, and re-layouts  16.7 us (10%)
  between operations  14.1 us (8%)
  other arithmetic  12 us (7%)
  blocking collectives  7.34 us (4%)
    all_gather x1, waiting for transfers between devices, per_device(): lax.all_gather(w_down, ('dp', 'ctx'), axis=0, tiled=True)  83.1 us
    all_gather x1, waiting for transfers between devices, per_device(): piece = lax.all_gather(kv_local, 'ctx', axis=0, tiled=True)  14.3 us
    dot_general x4, matrix products, update(): jnp.einsum('kgsd,tkd->kgst', query_heads, key_block, preferred_element_ty...  8.83 us
    dot_general x4, matrix products, update(): jnp.einsum('kgst,tkd->kgsd', expo.astype(jnp.bfloat16), value_block, pref...  8.43 us
    unnamed x1, blocking collectives  7.34 us
    dot_general x1, matrix products, per_device(): jnp.dot(latent, w_up, preferred_element_type=jnp.float32)  5.84 us
    dynamic_slice x12, local copies, waits for them, and re-layouts, per_device(): result, unused = lax.scan(step_block, start_state, (blocks, key_positions))  5.19 us
    while x20, local copies, waits for them, and re-layouts  5.18 us
  transfers between devices with their start and end apart: 2, of which 2 were waited for; matrix products, arithmetic and copies ran while one was open for 3% of the time, Pallas kernels for 0%

commit v1 on v0

--- a/solution.py
+++ b/solution.py
@@ -7,6 +7,13 @@
 QH = 32
 KVH = 4
 HD = 128
+
+
+def _pass_stacks_all(x_part, join_dim):
+    outcome_arr = list(x_part.shape[1:])
+    outcome_arr[join_dim] *= x_part.shape[0]
+    then = jnp.moveaxis(x_part, 0, join_dim).reshape(outcome_arr)
+    return then
 
 
 def per_device(tokens, w_down, w_up, queries, block_order):
@@ -59,7 +66,27 @@
         jnp.zeros((KVH, group, local_rows, HD), jnp.float32),
     )
     kv_local = jnp.dot(latent, w_up, preferred_element_type=jnp.float32).astype(jnp.bfloat16)
-    piece = lax.all_gather(kv_local, "ctx", axis=0, tiled=True)
+    n_dev_all = lax.psum(1, axis_name="ctx")
+    pages = []
+    for rr in [*range(n_dev_all)]:
+        pages.append((rr, (rr + 1) % n_dev_all))
+    by_rank = []
+    for u, num in pages:
+        by_rank.append((num, u))
+    w_next, u_next = ([], [])
+    for b in tuple(range(n_dev_all - 1)):
+        if b % 2 == 0:
+            w_next.append(
+                lax.ppermute(w_next[-1] if w_next else kv_local, axis_name="ctx", perm=pages)
+            )
+        else:
+            u_next.append(
+                lax.ppermute(u_next[-1] if u_next else kv_local, perm=by_rank, axis_name="ctx")
+            )
+    arr_out = jnp.stack([*w_next[::-1], kv_local, *u_next], axis=0)
+    moved = lax.axis_index("ctx") - len(w_next)
+    arr_out = arr_out[(jnp.arange(n_dev_all) - moved) % n_dev_all]
+    piece = _pass_stacks_all(arr_out, 0)
     count = piece.shape[0]
     width = math.gcd(count, 256)
     blocks = piece.reshape(count // width, width, piece.shape[1])

time: 172 us -> 197 us (1.15)
  local copies, waits for them, and re-layouts: 16.7 us -> 33.9 us
  starting transfers between devices: 0.04 us -> 6.59 us
    ppermute x0 -> x7, waiting for transfers between devices: none -> 14.9 us  [the longest x3 8.1 us: per_device(): lax.ppermute(u_next[-1] if u_next else kv_local, perm=by_rank, axis_name=...]
    all_gather x1 -> x0, waiting for transfers between devices: 14.3 us -> none  [per_device(): piece = lax.all_gather(kv_local, 'ctx', axis=0, tiled=True)]
    unnamed x11 -> x22, local copies, waits for them, and re-layouts: 3.63 us -> 14.4 us
    ppermute x0 -> x7, starting transfers between devices: none -> 6.59 us  [the longest x3 6.02 us: per_device(): lax.ppermute(u_next[-1] if u_next else kv_local, perm=by_rank, axis_name=...]
    gather x0 -> x1, local copies, waits for them, and re-layouts: none -> 3.59 us  [per_device(): arr_out = arr_out[(jnp.arange(n_dev_all) - moved) % n_dev_all]]
    while x20, local copies, waits for them, and re-layouts: 5.18 us -> 7.22 us
  transfers between devices with their start and end apart: 2 -> 8, of which waited for: 2 -> 6; matrix products, arithmetic and copies ran while one was open for 3% -> 8% of each run, Pallas kernels for 0% -> 0%
where the time goes in v1:
time: 197 us; the launch traced here: 196 us
  waiting for transfers between devices  98.7 us (50%)
  local copies, waits for them, and re-layouts  33.9 us (17%)
  matrix products  21.8 us (11%)
  between operations  14.2 us (7%)
  other arithmetic  11.9 us (6%)
  blocking collectives  8.22 us (4%)
  starting transfers between devices  6.59 us (3%)
    all_gather x1, waiting for transfers between devices, per_device(): lax.all_gather(w_down, ('dp', 'ctx'), axis=0, tiled=True)  83.1 us
    unnamed x22, local copies, waits for them, and re-layouts  14.4 us
    dot_general x4, matrix products, update(): jnp.einsum('kgst,tkd->kgsd', expo.astype(jnp.bfloat16), value_block, pref...  8.42 us
    dot_general x4, matrix products, update(): jnp.einsum('kgsd,tkd->kgst', query_heads, key_block, preferred_element_ty...  8.22 us
    unnamed x1, blocking collectives  8.22 us
    ppermute x3, waiting for transfers between devices, per_device(): lax.ppermute(u_next[-1] if u_next else kv_local, perm=by_rank, axis_name=...  8.1 us
    while x20, local copies, waits for them, and re-layouts  7.22 us
    ppermute x4, waiting for transfers between devices, per_device(): lax.ppermute(w_next[-1] if w_next else kv_local, axis_name='ctx', perm=pa...  6.79 us
  transfers between devices with their start and end apart: 8, of which 6 were waited for; matrix products, arithmetic and copies ran while one was open for 8% of the time, Pallas kernels for 0%

profile of v1, /device:TPU:0, one launch (start us, length us, event | category | flops | bytes accessed | tf_op | source)
XLA Modules:
  0.0 195.7 jit_solution(17988777057026347140)
XLA Ops:
  7.3 83.1 %all-gather.2.cloned.1.call-done = bf16[8192,512]{1,0:T(8,128)(2,1)} async-done(((bf16[256,512]{1,0:T(8,128)(2,1)}), bf16[8192,512]{1,0:T(8,128)(2,1)}) %all-gather.2.cloned.1.call-update) | async-done | bytes 8388624 | tf_op jit(solution)/shard_map/all_gather | solution.py:25
  90.4 5.1 %convolution_convert_fusion = bf16[128,1024]{1,0:T(8,128)(2,1)S(1)} fusion(bf16[512,1024]{1,0:T(8,128)(2,1)} %param.9, bf16[8192,512]{1,0:T(8,128)(2,1)} %all-gather.2.cloned.1.call-done, bf16[1,128,8192]{2,1,0:T(8,128)(2,1)S(1)} %copy-done), kind=kOutput, calls=%fused_computation.32 | convolution fusion | flops 1208156160 | bytes 11796480 | tf_op jit(solution)/shard_map/dot_general | solution.py:68
  97.2 5.1 %collective-permute-done = bf16[128,1024]{1,0:T(8,128)(2,1)S(1)} collective-permute-done((bf16[128,1024]{1,0:T(8,128)(2,1)S(1)}, bf16[128,1024]{1,0:T(8,128)(2,1)S(1)}, u32[]{:S(2)}, u32[]{:S(2)}) %collective-permute-start) | collective-permute-done | bytes 262176 | tf_op jit(solution)/shard_map/ppermute | solution.py:80
  102.3 8.2 %all-reduce = s32[16]{0:T(128)S(1)} all-reduce(s32[16]{0:T(128)S(1)} %bitcast_dynamic-update-slice_fusion.8), channel_id=1, replica_groups=mesh['dp'=4,'ctx'=8] {'ctx'}, use_global_device_ids=true, to_apply=%add | all-reduce | flops 16 | bytes 128
  111.8 5.5 %collective-permute-done.4 = bf16[128,1024]{1,0:T(8,128)(2,1)} collective-permute-done((bf16[128,1024]{1,0:T(8,128)(2,1)S(1)}, bf16[128,1024]{1,0:T(8,128)(2,1)}, u32[]{:S(2)}, u32[]{:S(2)}) %collective-permute-start.4) | collective-permute-done | bytes 262176 | tf_op jit(solution)/shard_map/ppermute | solution.py:84
  117.3 2.9 %collective-permute-start.5 = (bf16[128,1024]{1,0:T(8,128)(2,1)}, bf16[128,1024]{1,0:T(8,128)(2,1)}, u32[]{:S(2)}, u32[]{:S(2)}) collective-permute-start(bf16[128,1024]{1,0:T(8,128)(2,1)} %collective-permute-done.4), channel_id=1, source_target_pairs={{1,0},{2,1},{3,2},{4,3},{5,4},{6,5},{7,6},{0,7},{9,8},{10,9},{11,1... | collective-permute-start | bytes 786440 | tf_op jit(solution)/shard_map/ppermute | solution.py:84
  120.3 0.9 collective-permute-done.2
  121.2 1.6 copy.18
  122.8 1.3 copy.20
  124.1 2.6 %collective-permute-done.5 = bf16[128,1024]{1,0:T(8,128)(2,1)} collective-permute-done((bf16[128,1024]{1,0:T(8,128)(2,1)}, bf16[128,1024]{1,0:T(8,128)(2,1)}, u32[]{:S(2)}, u32[]{:S(2)}) %collective-permute-start.5) | collective-permute-done | bytes 262176 | tf_op jit(solution)/shard_map/ppermute | solution.py:84
  126.7 2.8 %collective-permute-start.6 = (bf16[128,1024]{1,0:T(8,128)(2,1)}, bf16[128,1024]{1,0:T(8,128)(2,1)S(1)}, u32[]{:S(2)}, u32[]{:S(2)}) collective-permute-start(bf16[128,1024]{1,0:T(8,128)(2,1)} %collective-permute-done.5), channel_id=1, source_target_pairs={{1,0},{2,1},{3,2},{4,3},{5,4},{6,5},{7,6},{0,7},{9,8},{10,9},{11,1... | collective-permute-start | bytes 786440 | tf_op jit(solution)/shard_map/ppermute | solution.py:84
  129.6 0.8 collective-permute-done.3
  130.4 1.7 bitcast_dynamic-update-slice_fusion.7
  132.1 1.7 bitcast_dynamic-update-slice_fusion.6
  133.7 1.7 bitcast_dynamic-update-slice_fusion.5
  135.4 1.7 bitcast_dynamic-update-slice_fusion.4
  137.1 0.7 bitcast_dynamic-update-slice_fusion.3
  137.8 1.7 bitcast_dynamic-update-slice_fusion.2
  139.5 1.7 bitcast_dynamic-update-slice_fusion.1
  141.2 0.7 bitcast_dynamic-update-slice_fusion
  141.9 3.6 %gather_fusion = bf16[8,128,1024]{2,1,0:T(8,128)(2,1)} fusion(bf16[8,128,1024]{2,1,0:T(8,128)(2,1)} %bitcast_dynamic-update-slice_fusion, s32[1024]{0:T(1024)S(1)} %pad_clamp_fusion), kind=kCustom, calls=%fused_computation | custom fusion | bytes 4194336 | tf_op jit(solution)/shard_map/gather | solution.py:88
  145.5 39.4 %while.15 = (s32[]{:T(128)}, f32[4,8,128]{2,1,0:T(8,128)S(1)}, f32[4,8,128]{2,1,0:T(8,128)S(1)}, f32[4,8,128,128]{3,2,1,0:T(8,128)}, s32[4,256]{1,0:T(4,128)S(1)...) while((s32[]{:T(128)}, f32[4,8,128]{2,1,0:T(8,128)S(1)}, ...), condition=%wide.region_4.5_spmd.clone, body=%wide.region_1.4_spmd.clone.sunk | while | flops 552129792 | bytes 38670536 | solution.py:103
  145.5 1.3 fusion.57
  146.9 1.1 constant_dynamic-slice_fusion.5
  148.2 2.1 %fusion.59 = (f32[4,8,128]{2,1,0:T(8,128)S(1)}, f32[4,256,8,128]{3,1,2,0:T(8,128)S(1)}) fusion(pred[128,256]{0,1:T(8,128)(4,1)S(1)} %broadcast_compare_fusion.2, bf16[256,4,128,1]{0,2,3,1:T(8,128)(2,1)S(1)} %bitcast.89, bf16[4,8,128,128]{3,2,1,0:T(8,128)(2,1)} %get-tuple-element.223), kind=kOutput, calls=%fused_computation.4.clone.1 | convolution fusion | flops 271577088 | bytes 5554176 | tf_op jit(solution)/shard_map/while/body/eval_jaxpr/kgsd,tkd->kgst/dot_general | solution.py:46
  150.3 1.1 fusion.60
  151.9 2.1 %fusion.62 = f32[4,8,128,128]{3,2,1,0:T(8,128)S(1)} fusion(f32[4,8,128,128]{3,2,1,0:T(8,128)S(1)} %copy-done.1, bf16[256,4,128,1]{0,2,3,1:T(8,128)(2,1)S(1)} %bitcast.91, f32[4,256,8,128]{3,1,2,0:T(8,128)S(1)} %get-tuple-element.191, f32[4,8,128]{2,1,0:T(8,128)S(1)} %select_maximum_fusion.2, pred[128,256]{0,1:T(8,128)(4,1)S(1)} %broadcast_compare_fusion.2, ...), kind=kOutput, calls=%fused_computation.9.clone.1 | convolution fusion | flops 275251200 | bytes 8716289 | tf_op jit(solution)/shard_map/while/body/eval_jaxpr/kgst,tkd->kgsd/dot_general | solution.py:55
  154.0 1.3 copy-done.2
  155.4 1.3 fusion.57
  156.7 1.1 constant_dynamic-slice_fusion.5
  158.1 2.1 %fusion.59 = (f32[4,8,128]{2,1,0:T(8,128)S(1)}, f32[4,256,8,128]{3,1,2,0:T(8,128)S(1)}) fusion(pred[128,256]{0,1:T(8,128)(4,1)S(1)} %broadcast_compare_fusion.2, bf16[256,4,128,1]{0,2,3,1:T(8,128)(2,1)S(1)} %bitcast.89, bf16[4,8,128,128]{3,2,1,0:T(8,128)(2,1)} %get-tuple-element.223), kind=kOutput, calls=%fused_computation.4.clone.1 | convolution fusion | flops 271577088 | bytes 5554176 | tf_op jit(solution)/shard_map/while/body/eval_jaxpr/kgsd,tkd->kgst/dot_general | solution.py:46
  160.2 1.1 fusion.60
  161.8 2.1 %fusion.62 = f32[4,8,128,128]{3,2,1,0:T(8,128)S(1)} fusion(f32[4,8,128,128]{3,2,1,0:T(8,128)S(1)} %copy-done.1, bf16[256,4,128,1]{0,2,3,1:T(8,128)(2,1)S(1)} %bitcast.91, f32[4,256,8,128]{3,1,2,0:T(8,128)S(1)} %get-tuple-element.191, f32[4,8,128]{2,1,0:T(8,128)S(1)} %select_maximum_fusion.2, pred[128,256]{0,1:T(8,128)(4,1)S(1)} %broadcast_compare_fusion.2, ...), kind=kOutput, calls=%fused_computation.9.clone.1 | convolution fusion | flops 275251200 | bytes 8716289 | tf_op jit(solution)/shard_map/while/body/eval_jaxpr/kgst,tkd->kgsd/dot_general | solution.py:55
  163.9 1.3 copy-done.2
  165.2 1.3 fusion.57
  166.6 1.1 constant_dynamic-slice_fusion.5
  167.9 2.1 %fusion.59 = (f32[4,8,128]{2,1,0:T(8,128)S(1)}, f32[4,256,8,128]{3,1,2,0:T(8,128)S(1)}) fusion(pred[128,256]{0,1:T(8,128)(4,1)S(1)} %broadcast_compare_fusion.2, bf16[256,4,128,1]{0,2,3,1:T(8,128)(2,1)S(1)} %bitcast.89, bf16[4,8,128,128]{3,2,1,0:T(8,128)(2,1)} %get-tuple-element.223), kind=kOutput, calls=%fused_computation.4.clone.1 | convolution fusion | flops 271577088 | bytes 5554176 | tf_op jit(solution)/shard_map/while/body/eval_jaxpr/kgsd,tkd->kgst/dot_general | solution.py:46
  170.0 1.1 fusion.60
  171.6 2.1 %fusion.62 = f32[4,8,128,128]{3,2,1,0:T(8,128)S(1)} fusion(f32[4,8,128,128]{3,2,1,0:T(8,128)S(1)} %copy-done.1, bf16[256,4,128,1]{0,2,3,1:T(8,128)(2,1)S(1)} %bitcast.91, f32[4,256,8,128]{3,1,2,0:T(8,128)S(1)} %get-tuple-element.191, f32[4,8,128]{2,1,0:T(8,128)S(1)} %select_maximum_fusion.2, pred[128,256]{0,1:T(8,128)(4,1)S(1)} %broadcast_compare_fusion.2, ...), kind=kOutput, calls=%fused_computation.9.clone.1 | convolution fusion | flops 275251200 | bytes 8716289 | tf_op jit(solution)/shard_map/while/body/eval_jaxpr/kgst,tkd->kgsd/dot_general | solution.py:55
  173.7 1.3 copy-done.2
  175.1 1.3 fusion.57
  176.5 1.1 constant_dynamic-slice_fusion.5
  177.8 2.1 %fusion.59 = (f32[4,8,128]{2,1,0:T(8,128)S(1)}, f32[4,256,8,128]{3,1,2,0:T(8,128)S(1)}) fusion(pred[128,256]{0,1:T(8,128)(4,1)S(1)} %broadcast_compare_fusion.2, bf16[256,4,128,1]{0,2,3,1:T(8,128)(2,1)S(1)} %bitcast.89, bf16[4,8,128,128]{3,2,1,0:T(8,128)(2,1)} %get-tuple-element.223), kind=kOutput, calls=%fused_computation.4.clone.1 | convolution fusion | flops 271577088 | bytes 5554176 | tf_op jit(solution)/shard_map/while/body/eval_jaxpr/kgsd,tkd->kgst/dot_general | solution.py:46
  179.9 1.1 fusion.60
  181.5 2.1 %fusion.62 = f32[4,8,128,128]{3,2,1,0:T(8,128)S(1)} fusion(f32[4,8,128,128]{3,2,1,0:T(8,128)S(1)} %copy-done.1, bf16[256,4,128,1]{0,2,3,1:T(8,128)(2,1)S(1)} %bitcast.91, f32[4,256,8,128]{3,1,2,0:T(8,128)S(1)} %get-tuple-element.191, f32[4,8,128]{2,1,0:T(8,128)S(1)} %select_maximum_fusion.2, pred[128,256]{0,1:T(8,128)(4,1)S(1)} %broadcast_compare_fusion.2, ...), kind=kOutput, calls=%fused_computation.9.clone.1 | convolution fusion | flops 275251200 | bytes 8716289 | tf_op jit(solution)/shard_map/while/body/eval_jaxpr/kgst,tkd->kgsd/dot_general | solution.py:55
  183.6 1.3 copy-done.2
  184.9 1.9 fusion.28
  187.6 1.3 convert_element_type.30
  (74 shorter events, 7.2 us)
Async XLA Ops:
  6.5 83.9 %copy-start = (bf16[1,128,8192]{2,1,0:T(8,128)(2,1)S(1)}, bf16[1,128,8192]{2,1,0:T(8,128)(2,1)}, u32[]{:S(2)}) copy-start(bf16[1,128,8192]{2,1,0:T(8,128)(2,1)} %param.7) | copy-start | bytes 6291460
  6.5 83.9 %all-gather.2.cloned.1.call-start = ((), (), s32[]{:S(2)}) async-start(), calls=%async_computation | async-start | bytes 8650752 | tf_op jit(solution)/shard_map/all_gather | solution.py:25
  7.3 88.6 %copy-start.6 = (u32[32]{0:T(128)S(1)}, u32[32]{0:T(128)}, u32[]{:S(2)}) copy-start(u32[32]{0:T(128)} %constant.94) | copy-start | bytes 388
  7.3 89.8 %copy-start.5 = (s32[1,2]{1,0:T(1,128)S(1)}, s32[1,2]{1,0:T(1,128)}, u32[]{:S(2)}) copy-start(s32[1,2]{1,0:T(1,128)} %param.11) | copy-start | bytes 28
  95.5 6.7 %collective-permute-start = (bf16[128,1024]{1,0:T(8,128)(2,1)S(1)}, bf16[128,1024]{1,0:T(8,128)(2,1)S(1)}, u32[]{:S(2)}, u32[]{:S(2)}) collective-permute-start(bf16[128,1024]{1,0:T(8,128)(2,1)S(1)} %convolution_convert_fusion), channel_id=1, source_target_pairs={{0,1},{1,2},{2,3},{3,4},{4,5},{5,6},{6,7},{7,0},{8,9},{9,10},{10,1... | collective-permute-start | bytes 786440 | tf_op jit(solution)/shard_map/ppermute | solution.py:80
  102.3 18.9 %copy-start.3 = (bf16[128,1024]{1,0:T(8,128)(2,1)}, bf16[128,1024]{1,0:T(8,128)(2,1)S(1)}, u32[]{:S(2)}) copy-start(bf16[128,1024]{1,0:T(8,128)(2,1)S(1)} %collective-permute-done) | copy-start | bytes 786436
  102.3 9.3 %collective-permute-start.1 = (bf16[128,1024]{1,0:T(8,128)(2,1)S(1)}, bf16[128,1024]{1,0:T(8,128)(2,1)S(1)}, u32[]{:S(2)}, u32[]{:S(2)}) collective-permute-start(bf16[128,1024]{1,0:T(8,128)(2,1)S(1)} %collective-permute-done), channel_id=1, source_target_pairs={{0,1},{1,2},{2,3},{3,4},{4,5},{5,6},{6,7},{7,0},{8,9},{9,10},{10,1... | collective-permute-start | bytes 786440 | tf_op jit(solution)/shard_map/ppermute | solution.py:80
  111.3 6.1 %collective-permute-start.4 = (bf16[128,1024]{1,0:T(8,128)(2,1)S(1)}, bf16[128,1024]{1,0:T(8,128)(2,1)}, u32[]{:S(2)}, u32[]{:S(2)}) collective-permute-start(bf16[128,1024]{1,0:T(8,128)(2,1)S(1)} %convolution_convert_fusion), channel_id=1, source_target_pairs={{1,0},{2,1},{3,2},{4,3},{5,4},{6,5},{7,6},{0,7},{9,8},{10,9},{11,1... | collective-permute-start | bytes 786440 | tf_op jit(solution)/shard_map/ppermute | solution.py:84
  111.6 9.6 %copy-start.4 = (bf16[128,1024]{1,0:T(8,128)(2,1)}, bf16[128,1024]{1,0:T(8,128)(2,1)S(1)}, u32[]{:S(2)}) copy-start(bf16[128,1024]{1,0:T(8,128)(2,1)S(1)} %collective-permute-done.1) | copy-start | bytes 786436
  111.6 9.6 %collective-permute-start.2 = (bf16[128,1024]{1,0:T(8,128)(2,1)S(1)}, bf16[128,1024]{1,0:T(8,128)(2,1)}, u32[]{:S(2)}, u32[]{:S(2)}) collective-permute-start(bf16[128,1024]{1,0:T(8,128)(2,1)S(1)} %collective-permute-done.1), channel_id=1, source_target_pairs={{0,1},{1,2},{2,3},{3,4},{4,5},{5,6},{6,7},{7,0},{8,9},{9,10},{10,1... | collective-permute-start | bytes 786440 | tf_op jit(solution)/shard_map/ppermute | solution.py:80
  117.3 9.4 %collective-permute-start.5 = (bf16[128,1024]{1,0:T(8,128)(2,1)}, bf16[128,1024]{1,0:T(8,128)(2,1)}, u32[]{:S(2)}, u32[]{:S(2)}) collective-permute-start(bf16[128,1024]{1,0:T(8,128)(2,1)} %collective-permute-done.4), channel_id=1, source_target_pairs={{1,0},{2,1},{3,2},{4,3},{5,4},{6,5},{7,6},{0,7},{9,8},{10,9},{11,1... | collective-permute-start | bytes 786440 | tf_op jit(solution)/shard_map/ppermute | solution.py:84
  121.1 9.3 %collective-permute-start.3 = (bf16[128,1024]{1,0:T(8,128)(2,1)}, bf16[128,1024]{1,0:T(8,128)(2,1)}, u32[]{:S(2)}, u32[]{:S(2)}) collective-permute-start(bf16[128,1024]{1,0:T(8,128)(2,1)} %collective-permute-done.2), channel_id=1, source_target_pairs={{0,1},{1,2},{2,3},{3,4},{4,5},{5,6},{6,7},{7,0},{8,9},{9,10},{10,1... | collective-permute-start | bytes 786440 | tf_op jit(solution)/shard_map/ppermute | solution.py:80
  126.7 14.4 %collective-permute-start.6 = (bf16[128,1024]{1,0:T(8,128)(2,1)}, bf16[128,1024]{1,0:T(8,128)(2,1)S(1)}, u32[]{:S(2)}, u32[]{:S(2)}) collective-permute-start(bf16[128,1024]{1,0:T(8,128)(2,1)} %collective-permute-done.5), channel_id=1, source_target_pairs={{1,0},{2,1},{3,2},{4,3},{5,4},{6,5},{7,6},{0,7},{9,8},{10,9},{11,1... | collective-permute-start | bytes 786440 | tf_op jit(solution)/shard_map/ppermute | solution.py:84
  150.3 1.6 copy-start.1
  154.0 1.3 copy-start.2
  160.2 1.6 copy-start.1
  163.9 1.3 copy-start.2
  170.0 1.6 copy-start.1
  173.7 1.3 copy-start.2
  179.9 1.6 copy-start.1
  183.6 1.3 copy-start.2
Sparse Core Ops, SparseCore 0:
  10.2 80.1 all-gather.1
